TPU v7x, 32 devices: a whole 2x2x4 slice. The times are simulated.
32 devices in a mesh: groups: 2 (over x), sample: 16 (over z, y, core).
Axes of the slice: x: 2, y: 2, z: 4, core: 2. Of those that a mesh axis runs over, the one named last changes fastest.
Arguments:
- prompt_states: bfloat16 [16384, 8192], P(('groups', 'sample')), parts along dimension 0, may hold values from -6 to 6
- page_table: int32 [128], P('groups'), parts along dimension 0, may hold values from 0 to 63, each once
- step_states: bfloat16 [2, 64, 8192], P(None, 'groups'), parts along dimension 1, may hold values from -15 to 15
- sample_order: int32 [64], P('groups'), parts along dimension 0, may hold values from 0 to 31, each once
- key_weight: bfloat16 [8192, 512], P('sample'), may hold values from -0.088388348 to 0.088388348
- value_weight: bfloat16 [8192, 512], P('sample'), may hold values from -0.0625 to 0.0625
- query_weight: bfloat16 [8192, 4096], P(None, 'sample'), may hold values from -0.121533978 to 0.121533978
- out_weight: bfloat16 [4096, 8192], P('sample'), may hold values from -0.125 to 0.125
Outputs:
- attn_out: bfloat16 [2, 64, 8192], P(None, 'groups', 'sample'), parts along dimension 1
There are 2 independent parts, one for each index of `groups`. A program takes and returns all parts, laid end to end along the dimension named above; an argument that names none is the same for every part. Nothing has to cross between parts.
Inputs may be any that keep to these rules, and one draw needn't show every extreme that they name: `page_table`: A permutation: entry p * 64 + j is the physical page that holds logical page j of prompt p; physical page r is rows r * 128 to (r + 1) * 128 - 1 of prompt_states. `sample_order`: A permutation; completion i continues prompt sample_order[i] // 32.
All inputs are finite; a program needn't handle non-finite values.
Results may differ from a plain program's by a relative error of at most 0.034.
Values may be sent and summed in bfloat16 or wider, within the bound.
A program may use at most 128 MiB of HBM per device.

v0:
```python
import jax
import jax.numpy as jnp
from jax import lax
from jax.sharding import PartitionSpec as P

D = 8192
HEAD_DIM = 128
KV_HEADS = 4
GQA = 8
PAGE = 128
PROMPT_PAGES = 64
rope_base = 1000000.0


def rotate(vector, position):
    half_dim = vector.shape[-1] // 2
    frequency = rope_base ** (-jnp.arange(half_dim, dtype=jnp.float32) * 2.0 / vector.shape[-1])
    angles = position.astype(jnp.float32)[..., None] * frequency
    cosine = jnp.cos(angles)
    sine_part = jnp.sin(angles)
    first_half = vector[..., :half_dim]
    second_half = vector[..., half_dim:]
    return jnp.concatenate(
        [
            first_half * cosine - second_half * sine_part,
            second_half * cosine + first_half * sine_part,
        ],
        axis=-1,
    )


def finish_heads(prefix_top, prefix_total, prefix_sum, queries, new_keys, new_values):
    score_scale = queries.shape[-1] ** (-0.5)
    query_wide = queries.astype(jnp.float32)
    key_wide = new_keys.astype(jnp.float32)
    value_wide = new_values.astype(jnp.float32)
    own_score = jnp.sum(query_wide * key_wide, axis=-1) * score_scale
    back_score = jnp.sum(query_wide[1] * key_wide[0], axis=-1) * score_scale
    first_high = jnp.maximum(prefix_top[0], own_score[0])
    first_old = jnp.exp(prefix_top[0] - first_high)
    first_own = jnp.exp(own_score[0] - first_high)
    first_out = (first_old[..., None] * prefix_sum[0] + first_own[..., None] * value_wide[0]) / (
        first_old * prefix_total[0] + first_own
    )[..., None]
    second_high = jnp.maximum(jnp.maximum(prefix_top[1], own_score[1]), back_score)
    second_old = jnp.exp(prefix_top[1] - second_high)
    second_back = jnp.exp(back_score - second_high)
    second_own = jnp.exp(own_score[1] - second_high)
    second_num = (
        second_old[..., None] * prefix_sum[1]
        + second_back[..., None] * value_wide[0]
        + second_own[..., None] * value_wide[1]
    )
    second_out = second_num / (second_old * prefix_total[1] + second_back + second_own)[..., None]
    return jnp.stack([first_out, second_out]).astype(jnp.bfloat16)


def on_device(
    prompt_states,
    page_table,
    step_states,
    sample_order,
    key_weight,
    value_weight,
    query_weight,
    out_weight,
):
    devices = lax.axis_size("sample")
    own_index = lax.axis_index("sample")
    row_count = prompt_states.shape[0]
    pages_here = row_count // PAGE
    heads_here = query_weight.shape[1] // HEAD_DIM
    total_pages = page_table.shape[0]
    prompts = total_pages // PROMPT_PAGES
    samples = sample_order.shape[0]
    group_size = samples // prompts
    score_scale = HEAD_DIM ** (-0.5)
    own_kv = own_index * heads_here // GQA
    slot_of = (
        jnp.zeros((total_pages,), jnp.int32)
        .at[page_table]
        .set(jnp.arange(total_pages, dtype=jnp.int32))
    )
    local_slots = lax.dynamic_slice_in_dim(slot_of, own_index * pages_here, pages_here)
    positions = (local_slots % PROMPT_PAGES * PAGE)[:, None] + jnp.arange(PAGE, dtype=jnp.int32)[
        None, :
    ]
    positions = positions.reshape(row_count)
    wide_states = step_states.reshape(2 * samples, D)
    key_piece = lax.all_gather(key_weight, "sample", axis=0, tiled=True)
    value_piece = lax.all_gather(value_weight, "sample", axis=0, tiled=True)
    piece_rows = key_piece.shape[0]
    key_acc = jnp.einsum(
        "rn,nkd->krd",
        prompt_states,
        key_piece.reshape(piece_rows, KV_HEADS, HEAD_DIM),
        preferred_element_type=jnp.float32,
    )
    value_acc = jnp.einsum(
        "rn,nkd->krd",
        prompt_states,
        value_piece.reshape(piece_rows, KV_HEADS, HEAD_DIM),
        preferred_element_type=jnp.float32,
    )
    key_head = lax.dynamic_slice_in_dim(key_piece, own_kv * HEAD_DIM, HEAD_DIM, 1)
    value_head = lax.dynamic_slice_in_dim(value_piece, own_kv * HEAD_DIM, HEAD_DIM, 1)
    key_step = jnp.dot(wide_states, key_head, preferred_element_type=jnp.float32)
    value_step = jnp.dot(wide_states, value_head, preferred_element_type=jnp.float32)
    key_acc, value_acc, key_step, value_step = (key_acc, value_acc, key_step, value_step)
    page_keys = rotate(key_acc, positions[None, :]).astype(jnp.bfloat16)
    page_values = value_acc.astype(jnp.bfloat16)
    step_place = (PROMPT_PAGES * PAGE + jnp.arange(2, dtype=jnp.int32))[:, None, None]
    queries = jnp.dot(wide_states, query_weight, preferred_element_type=jnp.float32).reshape(
        2, samples, heads_here, HEAD_DIM
    )
    queries = rotate(queries, step_place).astype(jnp.bfloat16)
    new_keys = rotate(key_step.reshape(2, samples, HEAD_DIM), step_place[:, :, 0]).astype(
        jnp.bfloat16
    )
    new_values = value_step.reshape(2, samples, HEAD_DIM).astype(jnp.bfloat16)
    inverse = (
        jnp.zeros((samples,), jnp.int32).at[sample_order].set(jnp.arange(samples, dtype=jnp.int32))
    )
    spread = devices // KV_HEADS
    send_keys = jnp.repeat(page_keys, spread, axis=0)
    send_values = jnp.repeat(page_values, spread, axis=0)
    all_keys, all_values = (
        lax.all_to_all(send_keys, "sample", split_axis=0, concat_axis=1, tiled=True),
        lax.all_to_all(send_values, "sample", split_axis=0, concat_axis=1, tiled=True),
    )
    logical = page_table.reshape(prompts, PROMPT_PAGES)
    all_keys = all_keys.reshape(total_pages, PAGE, HEAD_DIM)[logical].reshape(
        prompts, PROMPT_PAGES * PAGE, HEAD_DIM
    )
    all_values = all_values.reshape(total_pages, PAGE, HEAD_DIM)[logical].reshape(
        prompts, PROMPT_PAGES * PAGE, HEAD_DIM
    )
    sorted_query = queries[:, inverse].reshape(2, prompts, group_size, heads_here, HEAD_DIM)
    scores = (
        jnp.einsum("spmhd,pld->spmhl", sorted_query, all_keys, preferred_element_type=jnp.float32)
        * score_scale
    )
    prefix_top = jnp.max(scores, axis=-1)
    weights = jnp.exp(scores - prefix_top[..., None])
    prefix_total = jnp.sum(weights, axis=-1)
    prefix_sum = jnp.einsum(
        "spmhl,pld->spmhd",
        weights.astype(jnp.bfloat16),
        all_values,
        preferred_element_type=jnp.float32,
    )
    prefix_top = prefix_top.reshape(2, samples, heads_here)[:, sample_order]
    prefix_total = prefix_total.reshape(2, samples, heads_here)[:, sample_order]
    prefix_sum = prefix_sum.reshape(2, samples, heads_here, HEAD_DIM)[:, sample_order]
    head_out = finish_heads(
        prefix_top,
        prefix_total,
        prefix_sum,
        queries,
        new_keys[:, :, None, :],
        new_values[:, :, None, :],
    )
    flat_heads = head_out.reshape(2, samples, heads_here * HEAD_DIM)
    head_terms = jnp.einsum(
        "srk,kd->srd", flat_heads, out_weight, preferred_element_type=jnp.float32
    )
    return lax.psum_scatter(
        head_terms.astype(jnp.bfloat16), "sample", scatter_dimension=2, tiled=True
    )


def solution(mesh):
    in_specs = (
        P(("groups", "sample"), None),
        P("groups"),
        P(None, "groups", None),
        P("groups"),
        P("sample", None),
        P("sample", None),
        P(None, "sample"),
        P("sample", None),
    )
    out_specs = P(None, "groups", "sample")
    return jax.shard_map(
        on_device, mesh=mesh, in_specs=in_specs, out_specs=out_specs, check_vma=False
    )
```

profile of v0, /device:TPU:0, one launch (start us, length us, event | category | flops | bytes accessed | tf_op | source)
XLA Modules:
  0.0 351.2 jit_solution(6273337491218514646)
XLA Ops:
  6.5 0.7 all-gather.3.cloned.1.call-update
  7.3 0.7 all-gather.5.cloned.1.call-update
  8.0 0.7 compare_select_fusion.2
  8.7 0.8 scatter_custom_fusion
  9.5 0.1 fusion.61
  9.6 0.5 multiply_cosine_fusion
  10.2 77.0 %all-gather.3.cloned.1.call-done = bf16[8192,512]{1,0:T(8,128)(2,1)} async-done(((bf16[512,512]{1,0:T(8,128)(2,1)}), bf16[8192,512]{1,0:T(8,128)(2,1)}) %all-gather.3.cloned.1.call-update) | async-done | bytes 8388624 | tf_op jit(solution)/shard_map/all_gather | solution.py:90
  87.2 11.5 %copy.36 = bf16[8192,512]{0,1:T(8,128)(2,1)} copy(bf16[8192,512]{1,0:T(8,128)(2,1)} %all-gather.3.cloned.1.call-done) | data formatting | bytes 16777216 | tf_op jit(solution)/shard_map/all_gather | solution.py:90
  98.6 9.5 %fusion.16 = f32[4,512,128]{1,2,0:T(8,128)S(1)} fusion(bf16[8192,4,128]{0,2,1:T(8,128)(2,1)} %bitcast.153, bf16[512,8192]{1,0:T(8,128)(2,1)} %param.8), kind=kOutput, calls=%fused_computation.26 | convolution fusion | flops 4294967296 | bytes 17825792 | tf_op jit(solution)/shard_map/rn,nkd->krd/dot_general | solution.py:93
  108.2 0.2 subtract_convert_fusion
  108.4 0.3 copy.37
  108.7 1.8 broadcast_in_dim.13
  110.5 3.7 %all-to-all-start = ((bf16[16,512,128]{2,1,0:T(8,128)(2,1)}), bf16[16,512,128]{2,1,0:T(8,128)(2,1)S(1)}, u32[]{:S(2)}, u32[]{:S(2)}) async-start(bf16[16,512,128]{2,1,0:T(8,128)(2,1)} %bitcast.4), calls=%async_computation | async-start | bytes 4194304 | tf_op jit(solution)/shard_map/all_to_all | solution.py:128
  114.2 6.4 %copy.61 = bf16[256,8192]{1,0:T(8,128)(2,1)} copy(bf16[256,8192]{0,1:T(8,128)(2,1)} %bitcast.158) | data formatting | bytes 8388608 | tf_op jit(solution)/shard_map/dot_general | solution.py:113
  120.6 0.1 multiply_cosine_fusion.1
  120.7 4.3 %fusion.37 = f32[2,32,2,128]{3,1,2,0:T(8,128)S(1)} fusion(bf16[2,128,8192,1]{2,1,0,3:T(8,128)(2,1)} %bitcast.152, bf16[2,32,8192]{2,1,0:T(8,128)(2,1)S(1)} %copy-done), kind=kOutput, calls=%fused_computation.33 | convolution fusion | flops 268435456 | bytes 5308416 | tf_op jit(solution)/shard_map/dot_general | solution.py:113
  125.1 69.1 %all-gather.5.cloned.1.call-done = bf16[8192,512]{1,0:T(8,128)(2,1)} async-done(((bf16[512,512]{1,0:T(8,128)(2,1)}), bf16[8192,512]{1,0:T(8,128)(2,1)}) %all-gather.5.cloned.1.call-update) | async-done | bytes 8388624 | tf_op jit(solution)/shard_map/all_gather | solution.py:91
  194.2 11.4 %copy.44 = bf16[8192,512]{0,1:T(8,128)(2,1)} copy(bf16[8192,512]{1,0:T(8,128)(2,1)} %all-gather.5.cloned.1.call-done) | data formatting | bytes 16777216 | tf_op jit(solution)/shard_map/all_gather | solution.py:91
  205.6 11.1 %fusion.22 = bf16[4,512,128]{1,2,0:T(8,128)(2,1)} fusion(bf16[8192,4,128]{0,2,1:T(8,128)(2,1)} %bitcast.154, bf16[512,8192]{1,0:T(8,128)(2,1)} %param.8), kind=kOutput, calls=%fused_computation.28 | convolution fusion | flops 4295229440 | bytes 17301504 | tf_op jit(solution)/shard_map/rn,nkd->krd/dot_general | solution.py:99
  216.7 2.1 copy.45
  218.7 2.8 broadcast_in_dim.17
  221.6 7.3 %all-to-all-start.1 = ((bf16[16,512,128]{2,1,0:T(8,128)(2,1)}), bf16[16,512,128]{2,1,0:T(8,128)(2,1)}, u32[]{:S(2)}, u32[]{:S(2)}) async-start(bf16[16,512,128]{2,1,0:T(8,128)(2,1)} %bitcast.26), calls=%async_computation.1 | async-start | bytes 4194304 | tf_op jit(solution)/shard_map/all_to_all | solution.py:129
  228.9 0.1 subtract_convert_fusion.1
  229.2 0.9 scatter_custom_fusion.1
  230.1 0.6 gather_fusion.1
  230.7 2.1 fusion.14
  233.1 0.1 fusion.43
  233.2 0.1 multiply_reduce_fusion
  233.3 2.1 fusion.34
  235.4 2.1 gather_fusion
  237.5 4.2 %fusion.77 = (f32[2,32,2]{1,2,0:T(2,128)S(1)}, f32[2,1,32,2,8192]{4,2,3,0,1:T(8,128)}) fusion(bf16[8192,128,1,1]{1,0,3,2:T(8,128)(2,1)} %bitcast.156, bf16[2,32,2,128]{3,2,0,1:T(2,128)(2,1)S(1)} %bitcast.163), kind=kOutput, calls=%fused_computation.111 | convolution fusion | flops 270532480 | bytes 6324736 | tf_op jit(solution)/shard_map/spmhd,pld->spmhl/dot_general | solution.py:140
  241.8 0.1 copy.41
  241.9 2.9 fusion.6
  244.8 0.1 copy.48
  244.9 0.6 gather_fusion.5
  245.7 0.6 gather_fusion.2
  246.5 0.1 copy.43
  246.6 0.1 copy.47
  246.7 0.1 copy.50
  246.8 0.1 copy.53
  246.9 0.1 copy.54
  247.1 22.9 %all-to-all-done.1 = bf16[16,512,128]{2,1,0:T(8,128)(2,1)} async-done(((bf16[16,512,128]{2,1,0:T(8,128)(2,1)}), bf16[16,512,128]{2,1,0:T(8,128)(2,1)}, u32[]{:S(2)}, u32[]{:S(2)}) %all-to-all-start.1) | async-done | bytes 2097184 | tf_op jit(solution)/shard_map/all_to_all | solution.py:129
  270.0 2.5 gather_fusion.3
  272.6 3.0 fusion.25
  275.6 0.6 gather_fusion.4
  276.3 0.3 fusion.50
  276.7 4.0 %convolution_convert_fusion = bf16[2,32,8192]{2,1,0:T(8,128)(2,1)} fusion(bf16[256,8192]{1,0:T(8,128)(2,1)} %param.15, bf16[1,32,256]{2,1,0:T(8,128)(2,1)S(1)} %stack.10, bf16[1,32,256]{2,1,0:T(8,128)(2,1)S(1)} %stack.9), kind=kOutput, calls=%fused_computation.10 | convolution fusion | flops 268976128 | bytes 5275648 | tf_op jit(solution)/shard_map/srk,kd->srd/dot_general | solution.py:164
  280.7 64.0 %reduce-scatter.2.cloned.1.call-done = bf16[2,32,512]{2,1,0:T(8,128)(2,1)} async-done(((bf16[2,32,8192]{2,1,0:T(8,128)(2,1)}), bf16[2,32,512]{2,1,0:T(8,128)(2,1)}) %reduce-scatter.2.cloned.1.call-update) | async-done | bytes 65552 | tf_op jit(solution)/shard_map/reduce_scatter | solution.py:167
  (39 shorter events, 1.3 us)
Async XLA Ops:
  6.5 114.2 %copy-start = (bf16[2,32,8192]{2,1,0:T(8,128)(2,1)S(1)}, bf16[2,32,8192]{2,1,0:T(8,128)(2,1)}, u32[]{:S(2)}) copy-start(bf16[2,32,8192]{2,1,0:T(8,128)(2,1)} %param.10) | copy-start | bytes 3145732
  6.5 80.6 %all-gather.3.cloned.1.call-start = ((), (), s32[]{:S(2)}) async-start(), calls=%async_computation.3 | async-start | bytes 8912896 | tf_op jit(solution)/shard_map/all_gather | solution.py:90
  7.3 186.9 %all-gather.5.cloned.1.call-start = ((), (), s32[]{:S(2)}) async-start(), calls=%async_computation.4 | async-start | bytes 8912896 | tf_op jit(solution)/shard_map/all_gather | solution.py:91
  110.5 108.3 %all-to-all-start = ((bf16[16,512,128]{2,1,0:T(8,128)(2,1)}), bf16[16,512,128]{2,1,0:T(8,128)(2,1)S(1)}, u32[]{:S(2)}, u32[]{:S(2)}) async-start(bf16[16,512,128]{2,1,0:T(8,128)(2,1)} %bitcast.4), calls=%async_computation | async-start | bytes 4194304 | tf_op jit(solution)/shard_map/all_to_all | solution.py:128
  216.7 12.5 %copy-start.1 = (s32[32]{0:T(128)S(1)}, s32[32]{0:T(128)}, u32[]{:S(2)}) copy-start(s32[32]{0:T(128)} %param.11) | copy-start | bytes 388
  221.6 48.4 %all-to-all-start.1 = ((bf16[16,512,128]{2,1,0:T(8,128)(2,1)}), bf16[16,512,128]{2,1,0:T(8,128)(2,1)}, u32[]{:S(2)}, u32[]{:S(2)}) async-start(bf16[16,512,128]{2,1,0:T(8,128)(2,1)} %bitcast.26), calls=%async_computation.1 | async-start | bytes 4194304 | tf_op jit(solution)/shard_map/all_to_all | solution.py:129
  228.9 115.8 %reduce-scatter.2.cloned.1.call-start = ((), (), s32[]{:S(2)}) async-start(), calls=%async_computation.5 | async-start | bytes 1114112 | tf_op jit(solution)/shard_map/reduce_scatter | solution.py:167
Sparse Core Ops, SparseCore 0:
  9.5 77.5 all-gather.2
  89.3 104.7 all-gather.4
  280.8 63.8 reduce-scatter.1
where the time goes:
time: 352 us; the launch traced here: 351 us
  waiting for transfers between devices  234 us (66%)
  local copies, waits for them, and re-layouts  46.4 us (13%)
  matrix products  40.4 us (11%)
  between operations  13.4 us (4%)
  starting transfers between devices  11.1 us (3%)
  other arithmetic  5.57 us (2%)
    all_gather x1, waiting for transfers between devices, on_device(): key_piece = lax.all_gather(key_weight, 'sample', axis=0, tiled=True)  77 us
    all_gather x1, waiting for transfers between devices, on_device(): value_piece = lax.all_gather(value_weight, 'sample', axis=0, tiled=True)  69.1 us
    reduce_scatter x1, waiting for transfers between devices, on_device(): lax.psum_scatter(head_terms.astype(jnp.bfloat16), 'sample', scatter_dimen...  64 us
    all_to_all x1, waiting for transfers between devices, on_device(): lax.all_to_all(send_values, 'sample', split_axis=0, concat_axis=1, tiled=...  22.9 us
    all_gather x1, local copies, waits for them, and re-layouts, on_device(): key_piece = lax.all_gather(key_weight, 'sample', axis=0, tiled=True)  11.5 us
    all_gather x1, local copies, waits for them, and re-layouts, on_device(): value_piece = lax.all_gather(value_weight, 'sample', axis=0, tiled=True)  11.4 us
    dot_general x1, matrix products, on_device(): jnp.einsum('rn,nkd->krd', prompt_states, value_piece.reshape(piece_rows,...  11.1 us
    dot_general x1, matrix products, on_device(): jnp.einsum('rn,nkd->krd', prompt_states, key_piece.reshape(piece_rows, KV...  9.54 us
  transfers between devices with their start and end apart: 5, of which 4 were waited for; matrix products, arithmetic and copies ran while one was open for 22% of the time, Pallas kernels for 0%

commit v1 on v0

--- a/solution.py
+++ b/solution.py
@@ -88,7 +88,14 @@
     positions = positions.reshape(row_count)
     wide_states = step_states.reshape(2 * samples, D)
     key_piece = lax.all_gather(key_weight, "sample", axis=0, tiled=True)
-    value_piece = lax.all_gather(value_weight, "sample", axis=0, tiled=True)
+    ring = [value_weight]
+    for hop in range(15):
+        ring.append(lax.ppermute(ring[-1], "sample", [(dev, (dev + 1) % 16) for dev in range(16)]))
+    value_piece = jnp.roll(
+        jnp.concatenate(ring[::-1], axis=0),
+        (lax.axis_index("sample") + 1) * ring[0].shape[0],
+        axis=0,
+    )
     piece_rows = key_piece.shape[0]
     key_acc = jnp.einsum(
         "rn,nkd->krd",

time: 352 us -> 481 us (1.37)
  waiting for transfers between devices: 234 us -> 299 us
  local copies, waits for them, and re-layouts: 46.4 us -> 105 us
    ppermute x0 -> x15, waiting for transfers between devices: none -> 198 us  [on_device(): lax.ppermute(ring[-1], 'sample', [(dev, (dev + 1) % 16) for dev in range(...]
    all_gather x1, waiting for transfers between devices: 77 us -> 0.02 us  [on_device(): key_piece = lax.all_gather(key_weight, 'sample', axis=0, tiled=True)]
    all_gather x1 -> x0, waiting for transfers between devices: 69.1 us -> none  [on_device(): value_piece = lax.all_gather(value_weight, 'sample', axis=0, tiled=True)]
    unnamed x4 -> x79, local copies, waits for them, and re-layouts: 0.01 us -> 49.7 us
    all_to_all x1, waiting for transfers between devices: 0.01 us -> 20.7 us  [on_device(): lax.all_to_all(send_keys, 'sample', split_axis=0, concat_axis=1, tiled=True)]
    dynamic_slice x0 -> x2, local copies, waits for them, and re-layouts: none -> 18.9 us  [on_device(): jnp.roll(jnp.concatenate(ring[::-1], axis=0), (lax.axis_index('sample') +...]
    all_gather x1 -> x0, local copies, waits for them, and re-layouts: 11.4 us -> none  [on_device(): value_piece = lax.all_gather(value_weight, 'sample', axis=0, tiled=True)]
    all_to_all x1, waiting for transfers between devices: 22.9 us -> 14.6 us  [on_device(): lax.all_to_all(send_values, 'sample', split_axis=0, concat_axis=1, tiled=...]
  transfers between devices with their start and end apart: 5 -> 19, of which waited for: 4 -> 18; matrix products, arithmetic and copies ran while one was open for 22% -> 25% of each run, Pallas kernels for 0% -> 0%
where the time goes in v1:
time: 481 us; the launch traced here: 479 us
  waiting for transfers between devices  299 us (62%)
  local copies, waits for them, and re-layouts  105 us (22%)
  matrix products  39.5 us (8%)
  starting transfers between devices  15.5 us (3%)
  between operations  13.8 us (3%)
  other arithmetic  5.74 us (1%)
    ppermute x15, waiting for transfers between devices, on_device(): lax.ppermute(ring[-1], 'sample', [(dev, (dev + 1) % 16) for dev in range(...  198 us
    reduce_scatter x1, waiting for transfers between devices, on_device(): lax.psum_scatter(head_terms.astype(jnp.bfloat16), 'sample', scatter_dimen...  65.5 us
    unnamed x79, local copies, waits for them, and re-layouts  49.7 us
    all_to_all x1, waiting for transfers between devices, on_device(): lax.all_to_all(send_keys, 'sample', split_axis=0, concat_axis=1, tiled=True)  20.7 us
    dynamic_slice x2, local copies, waits for them, and re-layouts, on_device(): jnp.roll(jnp.concatenate(ring[::-1], axis=0), (lax.axis_index('sample') +...  18.9 us
    all_to_all x1, waiting for transfers between devices, on_device(): lax.all_to_all(send_values, 'sample', split_axis=0, concat_axis=1, tiled=...  14.6 us
    all_gather x1, local copies, waits for them, and re-layouts, on_device(): key_piece = lax.all_gather(key_weight, 'sample', axis=0, tiled=True)  12 us
    all_to_all x1, starting transfers between devices, on_device(): lax.all_to_all(send_keys, 'sample', split_axis=0, concat_axis=1, tiled=True)  11.2 us
  transfers between devices with their start and end apart: 19, of which 18 were waited for; matrix products, arithmetic and copies ran while one was open for 25% of the time, Pallas kernels for 0%

profile of v1, /device:TPU:0, one launch (start us, length us, event | category | flops | bytes accessed | tf_op | source)
XLA Modules:
  0.0 478.6 jit_solution(3470243943868632162)
XLA Ops:
  7.0 12.1 %collective-permute-done = bf16[512,512]{1,0:T(8,128)(2,1)S(1)} collective-permute-done((bf16[512,512]{1,0:T(8,128)(2,1)}, bf16[512,512]{1,0:T(8,128)(2,1)S(1)}, u32[]{:S(2)}, u32[]{:S(2)}) %collective-permute-start) | collective-permute-done | bytes 524320 | tf_op jit(solution)/shard_map/ppermute | solution.py:93
  19.1 11.3 %collective-permute-done.1 = bf16[512,512]{1,0:T(8,128)(2,1)S(1)} collective-permute-done((bf16[512,512]{1,0:T(8,128)(2,1)S(1)}, bf16[512,512]{1,0:T(8,128)(2,1)S(1)}, u32[]{:S(2)}, u32[]{:S(2)}) %collective-permute-start.1) | collective-permute-done | bytes 524320 | tf_op jit(solution)/shard_map/ppermute | solution.py:93
  30.4 22.4 %collective-permute-done.2 = bf16[512,512]{1,0:T(8,128)(2,1)S(1)} collective-permute-done((bf16[512,512]{1,0:T(8,128)(2,1)S(1)}, bf16[512,512]{1,0:T(8,128)(2,1)S(1)}, u32[]{:S(2)}, u32[]{:S(2)}) %collective-permute-start.2) | collective-permute-done | bytes 524320 | tf_op jit(solution)/shard_map/ppermute | solution.py:93
  52.8 11.5 %collective-permute-done.3 = bf16[512,512]{1,0:T(8,128)(2,1)S(1)} collective-permute-done((bf16[512,512]{1,0:T(8,128)(2,1)S(1)}, bf16[512,512]{1,0:T(8,128)(2,1)S(1)}, u32[]{:S(2)}, u32[]{:S(2)}) %collective-permute-start.3) | collective-permute-done | bytes 524320 | tf_op jit(solution)/shard_map/ppermute | solution.py:93
  65.1 22.5 %collective-permute-done.4 = bf16[512,512]{1,0:T(8,128)(2,1)S(1)} collective-permute-done((bf16[512,512]{1,0:T(8,128)(2,1)S(1)}, bf16[512,512]{1,0:T(8,128)(2,1)S(1)}, u32[]{:S(2)}, u32[]{:S(2)}) %collective-permute-start.4) | collective-permute-done | bytes 524320 | tf_op jit(solution)/shard_map/ppermute | solution.py:93
  88.4 16.1 %collective-permute-done.5 = bf16[512,512]{1,0:T(8,128)(2,1)S(1)} collective-permute-done((bf16[512,512]{1,0:T(8,128)(2,1)S(1)}, bf16[512,512]{1,0:T(8,128)(2,1)S(1)}, u32[]{:S(2)}, u32[]{:S(2)}) %collective-permute-start.5) | collective-permute-done | bytes 524320 | tf_op jit(solution)/shard_map/ppermute | solution.py:93
  105.3 11.4 %collective-permute-done.6 = bf16[512,512]{1,0:T(8,128)(2,1)S(1)} collective-permute-done((bf16[512,512]{1,0:T(8,128)(2,1)S(1)}, bf16[512,512]{1,0:T(8,128)(2,1)S(1)}, u32[]{:S(2)}, u32[]{:S(2)}) %collective-permute-start.6) | collective-permute-done | bytes 524320 | tf_op jit(solution)/shard_map/ppermute | solution.py:93
  117.5 11.3 %collective-permute-done.7 = bf16[512,512]{1,0:T(8,128)(2,1)S(1)} collective-permute-done((bf16[512,512]{1,0:T(8,128)(2,1)S(1)}, bf16[512,512]{1,0:T(8,128)(2,1)S(1)}, u32[]{:S(2)}, u32[]{:S(2)}) %collective-permute-start.7) | collective-permute-done | bytes 524320 | tf_op jit(solution)/shard_map/ppermute | solution.py:93
  129.6 11.3 %collective-permute-done.8 = bf16[512,512]{1,0:T(8,128)(2,1)S(1)} collective-permute-done((bf16[512,512]{1,0:T(8,128)(2,1)S(1)}, bf16[512,512]{1,0:T(8,128)(2,1)S(1)}, u32[]{:S(2)}, u32[]{:S(2)}) %collective-permute-start.8) | collective-permute-done | bytes 524320 | tf_op jit(solution)/shard_map/ppermute | solution.py:93
  141.7 11.3 %collective-permute-done.9 = bf16[512,512]{1,0:T(8,128)(2,1)S(1)} collective-permute-done((bf16[512,512]{1,0:T(8,128)(2,1)S(1)}, bf16[512,512]{1,0:T(8,128)(2,1)S(1)}, u32[]{:S(2)}, u32[]{:S(2)}) %collective-permute-start.9) | collective-permute-done | bytes 524320 | tf_op jit(solution)/shard_map/ppermute | solution.py:93
  153.8 11.3 %collective-permute-done.10 = bf16[512,512]{1,0:T(8,128)(2,1)S(1)} collective-permute-done((bf16[512,512]{1,0:T(8,128)(2,1)S(1)}, bf16[512,512]{1,0:T(8,128)(2,1)S(1)}, u32[]{:S(2)}, u32[]{:S(2)}) %collective-permute-start.10) | collective-permute-done | bytes 524320 | tf_op jit(solution)/shard_map/ppermute | solution.py:93
  165.9 11.3 %collective-permute-done.11 = bf16[512,512]{1,0:T(8,128)(2,1)S(1)} collective-permute-done((bf16[512,512]{1,0:T(8,128)(2,1)S(1)}, bf16[512,512]{1,0:T(8,128)(2,1)S(1)}, u32[]{:S(2)}, u32[]{:S(2)}) %collective-permute-start.11) | collective-permute-done | bytes 524320 | tf_op jit(solution)/shard_map/ppermute | solution.py:93
  178.1 11.3 %collective-permute-done.12 = bf16[512,512]{1,0:T(8,128)(2,1)S(1)} collective-permute-done((bf16[512,512]{1,0:T(8,128)(2,1)S(1)}, bf16[512,512]{1,0:T(8,128)(2,1)S(1)}, u32[]{:S(2)}, u32[]{:S(2)}) %collective-permute-start.12) | collective-permute-done | bytes 524320 | tf_op jit(solution)/shard_map/ppermute | solution.py:93
  190.2 11.4 %collective-permute-done.13 = bf16[512,512]{1,0:T(8,128)(2,1)} collective-permute-done((bf16[512,512]{1,0:T(8,128)(2,1)S(1)}, bf16[512,512]{1,0:T(8,128)(2,1)}, u32[]{:S(2)}, u32[]{:S(2)}) %collective-permute-start.13) | collective-permute-done | bytes 524320 | tf_op jit(solution)/shard_map/ppermute | solution.py:93
  201.7 11.5 %collective-permute-done.14 = bf16[512,512]{1,0:T(8,128)(2,1)} collective-permute-done((bf16[512,512]{1,0:T(8,128)(2,1)}, bf16[512,512]{1,0:T(8,128)(2,1)}, u32[]{:S(2)}, u32[]{:S(2)}) %collective-permute-start.14) | collective-permute-done | bytes 524320 | tf_op jit(solution)/shard_map/ppermute | solution.py:93
  215.1 1.9 constant_dynamic-update-slice_fusion.30
  220.7 1.9 constant_dynamic-update-slice_fusion.27
  222.6 1.9 constant_dynamic-update-slice_fusion.26
  224.5 1.9 constant_dynamic-update-slice_fusion.25
  226.3 1.9 constant_dynamic-update-slice_fusion.24
  228.2 1.9 constant_dynamic-update-slice_fusion.23
  230.1 1.9 constant_dynamic-update-slice_fusion.22
  233.8 1.9 constant_dynamic-update-slice_fusion.20
  238.3 1.9 constant_dynamic-update-slice_fusion.16
  240.2 1.9 constant_dynamic-update-slice_fusion.15
  242.1 1.9 constant_dynamic-update-slice_fusion.14
  255.7 7.2 %constant_dynamic-slice_fusion = bf16[8192,512]{1,0:T(8,128)(2,1)} fusion(bf16[16384,512]{1,0:T(8,128)(2,1)} %constant_dynamic-update-slice_fusion, s32[]{:T(128)S(6)} %select_n.57), kind=kLoop, calls=%fused_computation.132 | loop fusion | bytes 16777220 | tf_op jit(solution)/shard_map/jit(_roll_dynamic)/dynamic_slice | solution.py:94
  262.9 11.7 %copy.44 = bf16[8192,512]{0,1:T(8,128)(2,1)} copy(bf16[8192,512]{1,0:T(8,128)(2,1)} %constant_dynamic-slice_fusion) | data formatting | bytes 16777216 | tf_op jit(solution)/shard_map/jit(_roll_dynamic)/dynamic_slice | solution.py:94
  274.6 10.3 %fusion.22 = bf16[4,512,128]{1,2,0:T(8,128)(2,1)S(1)} fusion(bf16[8192,4,128]{0,2,1:T(8,128)(2,1)} %bitcast.153, bf16[512,8192]{1,0:T(8,128)(2,1)} %param.8), kind=kOutput, calls=%fused_computation.28 | convolution fusion | flops 4295229440 | bytes 17301504 | tf_op jit(solution)/shard_map/rn,nkd->krd/dot_general | solution.py:106
  286.9 3.7 all-to-all-start.1
  292.4 12.0 %copy.36 = bf16[8192,512]{0,1:T(8,128)(2,1)} copy(bf16[8192,512]{1,0:T(8,128)(2,1)} %all-gather.2.cloned.1.call-done) | data formatting | bytes 16777216 | tf_op jit(solution)/shard_map/all_gather | solution.py:90
  304.4 9.5 %fusion.16 = f32[4,512,128]{1,2,0:T(8,128)S(1)} fusion(bf16[8192,4,128]{0,2,1:T(8,128)(2,1)} %bitcast.154, bf16[512,8192]{1,0:T(8,128)(2,1)} %param.8), kind=kOutput, calls=%fused_computation.26 | convolution fusion | flops 4294967296 | bytes 17825792 | tf_op jit(solution)/shard_map/rn,nkd->krd/dot_general | solution.py:100
  315.0 2.0 copy.37
  317.1 14.6 %all-to-all-done.1 = bf16[16,512,128]{2,1,0:T(8,128)(2,1)S(1)} async-done(((bf16[16,512,128]{2,1,0:T(8,128)(2,1)}), bf16[16,512,128]{2,1,0:T(8,128)(2,1)S(1)}, u32[]{:S(2)}, u32[]{:S(2)}) %all-to-all-start.1) | async-done | bytes 2097184 | tf_op jit(solution)/shard_map/all_to_all | solution.py:136
  331.7 2.8 broadcast_in_dim.13
  334.5 11.2 %all-to-all-start = ((bf16[16,512,128]{2,1,0:T(8,128)(2,1)}), bf16[16,512,128]{2,1,0:T(8,128)(2,1)}, u32[]{:S(2)}, u32[]{:S(2)}) async-start(bf16[16,512,128]{2,1,0:T(8,128)(2,1)} %bitcast.4), calls=%async_computation | async-start | bytes 4194304 | tf_op jit(solution)/shard_map/all_to_all | solution.py:135
  345.8 6.4 %copy.61 = bf16[256,8192]{1,0:T(8,128)(2,1)} copy(bf16[256,8192]{0,1:T(8,128)(2,1)} %bitcast.158) | data formatting | bytes 8388608 | tf_op jit(solution)/shard_map/dot_general | solution.py:120
  352.4 3.6 fusion.37
  357.8 3.7 fusion.34
  361.5 2.2 gather_fusion.3
  363.7 2.1 fusion.14
  366.2 20.7 %all-to-all-done = bf16[16,512,128]{2,1,0:T(8,128)(2,1)} async-done(((bf16[16,512,128]{2,1,0:T(8,128)(2,1)}), bf16[16,512,128]{2,1,0:T(8,128)(2,1)}, u32[]{:S(2)}, u32[]{:S(2)}) %all-to-all-start) | async-done | bytes 2097184 | tf_op jit(solution)/shard_map/all_to_all | solution.py:135
  386.9 2.5 gather_fusion
  389.4 2.7 fusion.76
  392.2 2.9 fusion.6
  395.1 3.7 fusion.25
  402.2 4.0 convolution_convert_fusion
  406.3 65.5 %reduce-scatter.2.cloned.1.call-done = bf16[2,32,512]{2,1,0:T(8,128)(2,1)} async-done(((bf16[2,32,8192]{2,1,0:T(8,128)(2,1)}), bf16[2,32,512]{2,1,0:T(8,128)(2,1)}) %reduce-scatter.2.cloned.1.call-update) | async-done | bytes 65552 | tf_op jit(solution)/shard_map/reduce_scatter | solution.py:174
  (142 shorter events, 40.9 us)
Async XLA Ops:
  6.5 345.8 %copy-start = (bf16[2,32,8192]{2,1,0:T(8,128)(2,1)S(1)}, bf16[2,32,8192]{2,1,0:T(8,128)(2,1)}, u32[]{:S(2)}) copy-start(bf16[2,32,8192]{2,1,0:T(8,128)(2,1)} %param.10) | copy-start | bytes 3145732
  6.5 248.3 %copy-start.1 = (bf16[512,512]{1,0:T(8,128)(2,1)S(1)}, bf16[512,512]{1,0:T(8,128)(2,1)}, u32[]{:S(2)}) copy-start(bf16[512,512]{1,0:T(8,128)(2,1)} %param.13) | copy-start | bytes 1572868
  6.5 285.8 %all-gather.2.cloned.1.call-start = ((), (), s32[]{:S(2)}) async-start(), calls=%async_computation.3 | async-start | bytes 8912896 | tf_op jit(solution)/shard_map/all_gather | solution.py:90
  6.5 12.5 %collective-permute-start = (bf16[512,512]{1,0:T(8,128)(2,1)}, bf16[512,512]{1,0:T(8,128)(2,1)S(1)}, u32[]{:S(2)}, u32[]{:S(2)}) collective-permute-start(bf16[512,512]{1,0:T(8,128)(2,1)} %param.13), channel_id=1, source_target_pairs={{0,1},{1,2},{2,3},{3,4},{4,5},{5,6},{6,7},{7,8},{8,9},{9,10},{10,1... | collective-permute-start | bytes 1572872 | tf_op jit(solution)/shard_map/ppermute | solution.py:93
  19.1 11.3 %collective-permute-start.1 = (bf16[512,512]{1,0:T(8,128)(2,1)S(1)}, bf16[512,512]{1,0:T(8,128)(2,1)S(1)}, u32[]{:S(2)}, u32[]{:S(2)}) collective-permute-start(bf16[512,512]{1,0:T(8,128)(2,1)S(1)} %collective-permute-done), channel_id=1, source_target_pairs={{0,1},{1,2},{2,3},{3,4},{4,5},{5,6},{6,7},{7,8},{8,9},{9,10},{10,1... | collective-permute-start | bytes 1572872 | tf_op jit(solution)/shard_map/ppermute | solution.py:93
  30.4 22.4 %collective-permute-start.2 = (bf16[512,512]{1,0:T(8,128)(2,1)S(1)}, bf16[512,512]{1,0:T(8,128)(2,1)S(1)}, u32[]{:S(2)}, u32[]{:S(2)}) collective-permute-start(bf16[512,512]{1,0:T(8,128)(2,1)S(1)} %collective-permute-done.1), channel_id=1, source_target_pairs={{0,1},{1,2},{2,3},{3,4},{4,5},{5,6},{6,7},{7,8},{8,9},{9,10},{10,1... | collective-permute-start | bytes 1572872 | tf_op jit(solution)/shard_map/ppermute | solution.py:93
  52.8 11.5 %collective-permute-start.3 = (bf16[512,512]{1,0:T(8,128)(2,1)S(1)}, bf16[512,512]{1,0:T(8,128)(2,1)S(1)}, u32[]{:S(2)}, u32[]{:S(2)}) collective-permute-start(bf16[512,512]{1,0:T(8,128)(2,1)S(1)} %collective-permute-done.2), channel_id=1, source_target_pairs={{0,1},{1,2},{2,3},{3,4},{4,5},{5,6},{6,7},{7,8},{8,9},{9,10},{10,1... | collective-permute-start | bytes 1572872 | tf_op jit(solution)/shard_map/ppermute | solution.py:93
  64.2 0.8 copy-start.2
  65.1 22.5 %collective-permute-start.4 = (bf16[512,512]{1,0:T(8,128)(2,1)S(1)}, bf16[512,512]{1,0:T(8,128)(2,1)S(1)}, u32[]{:S(2)}, u32[]{:S(2)}) collective-permute-start(bf16[512,512]{1,0:T(8,128)(2,1)S(1)} %collective-permute-done.3), channel_id=1, source_target_pairs={{0,1},{1,2},{2,3},{3,4},{4,5},{5,6},{6,7},{7,8},{8,9},{9,10},{10,1... | collective-permute-start | bytes 1572872 | tf_op jit(solution)/shard_map/ppermute | solution.py:93
  87.6 0.8 copy-start.4
  88.4 16.1 %collective-permute-start.5 = (bf16[512,512]{1,0:T(8,128)(2,1)S(1)}, bf16[512,512]{1,0:T(8,128)(2,1)S(1)}, u32[]{:S(2)}, u32[]{:S(2)}) collective-permute-start(bf16[512,512]{1,0:T(8,128)(2,1)S(1)} %collective-permute-done.4), channel_id=1, source_target_pairs={{0,1},{1,2},{2,3},{3,4},{4,5},{5,6},{6,7},{7,8},{8,9},{9,10},{10,1... | collective-permute-start | bytes 1572872 | tf_op jit(solution)/shard_map/ppermute | solution.py:93
  104.5 0.8 copy-start.6
  105.3 11.4 %collective-permute-start.6 = (bf16[512,512]{1,0:T(8,128)(2,1)S(1)}, bf16[512,512]{1,0:T(8,128)(2,1)S(1)}, u32[]{:S(2)}, u32[]{:S(2)}) collective-permute-start(bf16[512,512]{1,0:T(8,128)(2,1)S(1)} %collective-permute-done.5), channel_id=1, source_target_pairs={{0,1},{1,2},{2,3},{3,4},{4,5},{5,6},{6,7},{7,8},{8,9},{9,10},{10,1... | collective-permute-start | bytes 1572872 | tf_op jit(solution)/shard_map/ppermute | solution.py:93
  116.7 0.8 copy-start.8
  117.5 11.3 %collective-permute-start.7 = (bf16[512,512]{1,0:T(8,128)(2,1)S(1)}, bf16[512,512]{1,0:T(8,128)(2,1)S(1)}, u32[]{:S(2)}, u32[]{:S(2)}) collective-permute-start(bf16[512,512]{1,0:T(8,128)(2,1)S(1)} %collective-permute-done.6), channel_id=1, source_target_pairs={{0,1},{1,2},{2,3},{3,4},{4,5},{5,6},{6,7},{7,8},{8,9},{9,10},{10,1... | collective-permute-start | bytes 1572872 | tf_op jit(solution)/shard_map/ppermute | solution.py:93
  128.8 0.8 copy-start.10
  129.6 11.3 %collective-permute-start.8 = (bf16[512,512]{1,0:T(8,128)(2,1)S(1)}, bf16[512,512]{1,0:T(8,128)(2,1)S(1)}, u32[]{:S(2)}, u32[]{:S(2)}) collective-permute-start(bf16[512,512]{1,0:T(8,128)(2,1)S(1)} %collective-permute-done.7), channel_id=1, source_target_pairs={{0,1},{1,2},{2,3},{3,4},{4,5},{5,6},{6,7},{7,8},{8,9},{9,10},{10,1... | collective-permute-start | bytes 1572872 | tf_op jit(solution)/shard_map/ppermute | solution.py:93
  140.9 0.8 copy-start.12
  141.7 11.3 %collective-permute-start.9 = (bf16[512,512]{1,0:T(8,128)(2,1)S(1)}, bf16[512,512]{1,0:T(8,128)(2,1)S(1)}, u32[]{:S(2)}, u32[]{:S(2)}) collective-permute-start(bf16[512,512]{1,0:T(8,128)(2,1)S(1)} %collective-permute-done.8), channel_id=1, source_target_pairs={{0,1},{1,2},{2,3},{3,4},{4,5},{5,6},{6,7},{7,8},{8,9},{9,10},{10,1... | collective-permute-start | bytes 1572872 | tf_op jit(solution)/shard_map/ppermute | solution.py:93
  153.0 0.8 copy-start.14
  153.8 11.3 %collective-permute-start.10 = (bf16[512,512]{1,0:T(8,128)(2,1)S(1)}, bf16[512,512]{1,0:T(8,128)(2,1)S(1)}, u32[]{:S(2)}, u32[]{:S(2)}) collective-permute-start(bf16[512,512]{1,0:T(8,128)(2,1)S(1)} %collective-permute-done.9), channel_id=1, source_target_pairs={{0,1},{1,2},{2,3},{3,4},{4,5},{5,6},{6,7},{7,8},{8,9},{9,10},{10,1... | collective-permute-start | bytes 1572872 | tf_op jit(solution)/shard_map/ppermute | solution.py:93
  165.1 0.8 copy-start.16
  165.9 11.3 %collective-permute-start.11 = (bf16[512,512]{1,0:T(8,128)(2,1)S(1)}, bf16[512,512]{1,0:T(8,128)(2,1)S(1)}, u32[]{:S(2)}, u32[]{:S(2)}) collective-permute-start(bf16[512,512]{1,0:T(8,128)(2,1)S(1)} %collective-permute-done.10), channel_id=1, source_target_pairs={{0,1},{1,2},{2,3},{3,4},{4,5},{5,6},{6,7},{7,8},{8,9},{9,10},{10,1... | collective-permute-start | bytes 1572872 | tf_op jit(solution)/shard_map/ppermute | solution.py:93
  177.2 0.8 copy-start.18
  178.1 11.3 %collective-permute-start.12 = (bf16[512,512]{1,0:T(8,128)(2,1)S(1)}, bf16[512,512]{1,0:T(8,128)(2,1)S(1)}, u32[]{:S(2)}, u32[]{:S(2)}) collective-permute-start(bf16[512,512]{1,0:T(8,128)(2,1)S(1)} %collective-permute-done.11), channel_id=1, source_target_pairs={{0,1},{1,2},{2,3},{3,4},{4,5},{5,6},{6,7},{7,8},{8,9},{9,10},{10,1... | collective-permute-start | bytes 1572872 | tf_op jit(solution)/shard_map/ppermute | solution.py:93
  189.4 0.8 copy-start.20
  190.2 11.4 %collective-permute-start.13 = (bf16[512,512]{1,0:T(8,128)(2,1)S(1)}, bf16[512,512]{1,0:T(8,128)(2,1)}, u32[]{:S(2)}, u32[]{:S(2)}) collective-permute-start(bf16[512,512]{1,0:T(8,128)(2,1)S(1)} %collective-permute-done.12), channel_id=1, source_target_pairs={{0,1},{1,2},{2,3},{3,4},{4,5},{5,6},{6,7},{7,8},{8,9},{9,10},{10,1... | collective-permute-start | bytes 1572872 | tf_op jit(solution)/shard_map/ppermute | solution.py:93
  201.6 11.6 %collective-permute-start.14 = (bf16[512,512]{1,0:T(8,128)(2,1)}, bf16[512,512]{1,0:T(8,128)(2,1)}, u32[]{:S(2)}, u32[]{:S(2)}) collective-permute-start(bf16[512,512]{1,0:T(8,128)(2,1)} %collective-permute-done.13), channel_id=1, source_target_pairs={{0,1},{1,2},{2,3},{3,4},{4,5},{5,6},{6,7},{7,8},{8,9},{9,10},{10,1... | collective-permute-start | bytes 1572872 | tf_op jit(solution)/shard_map/ppermute | solution.py:93
  201.6 42.4 %copy-start.21 = (bf16[512,512]{1,0:T(8,128)(2,1)S(1)}, bf16[512,512]{1,0:T(8,128)(2,1)}, u32[]{:S(2)}) copy-start(bf16[512,512]{1,0:T(8,128)(2,1)} %copy-done.20) | copy-start | bytes 1572868
  201.6 43.2 %copy-start.19 = (bf16[512,512]{1,0:T(8,128)(2,1)S(1)}, bf16[512,512]{1,0:T(8,128)(2,1)}, u32[]{:S(2)}) copy-start(bf16[512,512]{1,0:T(8,128)(2,1)} %copy-done.18) | copy-start | bytes 1572868
  201.6 44.0 %copy-start.17 = (bf16[512,512]{1,0:T(8,128)(2,1)S(1)}, bf16[512,512]{1,0:T(8,128)(2,1)}, u32[]{:S(2)}) copy-start(bf16[512,512]{1,0:T(8,128)(2,1)} %copy-done.16) | copy-start | bytes 1572868
  201.6 44.9 %copy-start.15 = (bf16[512,512]{1,0:T(8,128)(2,1)S(1)}, bf16[512,512]{1,0:T(8,128)(2,1)}, u32[]{:S(2)}) copy-start(bf16[512,512]{1,0:T(8,128)(2,1)} %copy-done.14) | copy-start | bytes 1572868
  201.6 45.7 %copy-start.13 = (bf16[512,512]{1,0:T(8,128)(2,1)S(1)}, bf16[512,512]{1,0:T(8,128)(2,1)}, u32[]{:S(2)}) copy-start(bf16[512,512]{1,0:T(8,128)(2,1)} %copy-done.12) | copy-start | bytes 1572868
  201.6 46.5 %copy-start.11 = (bf16[512,512]{1,0:T(8,128)(2,1)S(1)}, bf16[512,512]{1,0:T(8,128)(2,1)}, u32[]{:S(2)}) copy-start(bf16[512,512]{1,0:T(8,128)(2,1)} %copy-done.10) | copy-start | bytes 1572868
  201.6 47.4 %copy-start.9 = (bf16[512,512]{1,0:T(8,128)(2,1)S(1)}, bf16[512,512]{1,0:T(8,128)(2,1)}, u32[]{:S(2)}) copy-start(bf16[512,512]{1,0:T(8,128)(2,1)} %copy-done.8) | copy-start | bytes 1572868
  201.6 48.2 %copy-start.7 = (bf16[512,512]{1,0:T(8,128)(2,1)S(1)}, bf16[512,512]{1,0:T(8,128)(2,1)}, u32[]{:S(2)}) copy-start(bf16[512,512]{1,0:T(8,128)(2,1)} %copy-done.6) | copy-start | bytes 1572868
  201.6 49.0 %copy-start.5 = (bf16[512,512]{1,0:T(8,128)(2,1)S(1)}, bf16[512,512]{1,0:T(8,128)(2,1)}, u32[]{:S(2)}) copy-start(bf16[512,512]{1,0:T(8,128)(2,1)} %copy-done.4) | copy-start | bytes 1572868
  201.7 49.8 %copy-start.3 = (bf16[512,512]{1,0:T(8,128)(2,1)S(1)}, bf16[512,512]{1,0:T(8,128)(2,1)}, u32[]{:S(2)}) copy-start(bf16[512,512]{1,0:T(8,128)(2,1)} %copy-done.2) | copy-start | bytes 1572868
  274.6 16.1 %copy-start.22 = (s32[64]{0:T(128)S(1)}, s32[64]{0:T(128)}, u32[]{:S(2)}) copy-start(s32[64]{0:T(128)} %param.9) | copy-start | bytes 772
  286.9 44.8 %all-to-all-start.1 = ((bf16[16,512,128]{2,1,0:T(8,128)(2,1)}), bf16[16,512,128]{2,1,0:T(8,128)(2,1)S(1)}, u32[]{:S(2)}, u32[]{:S(2)}) async-start(bf16[16,512,128]{2,1,0:T(8,128)(2,1)} %bitcast.26), calls=%async_computation.1 | async-start | bytes 4194304 | tf_op jit(solution)/shard_map/all_to_all | solution.py:136
  313.9 42.2 %copy-start.23 = (s32[32]{0:T(128)S(1)}, s32[32]{0:T(128)}, u32[]{:S(2)}) copy-start(s32[32]{0:T(128)} %param.11) | copy-start | bytes 388
  334.5 52.4 %all-to-all-start = ((bf16[16,512,128]{2,1,0:T(8,128)(2,1)}), bf16[16,512,128]{2,1,0:T(8,128)(2,1)}, u32[]{:S(2)}, u32[]{:S(2)}) async-start(bf16[16,512,128]{2,1,0:T(8,128)(2,1)} %bitcast.4), calls=%async_computation | async-start | bytes 4194304 | tf_op jit(solution)/shard_map/all_to_all | solution.py:135
  345.7 126.0 %reduce-scatter.2.cloned.1.call-start = ((), (), s32[]{:S(2)}) async-start(), calls=%async_computation.4 | async-start | bytes 1114112 | tf_op jit(solution)/shard_map/reduce_scatter | solution.py:174
Sparse Core Ops, SparseCore 0:
  19.2 88.5 all-gather.1
  406.4 65.2 reduce-scatter.1
